TPU v7x, 512 devices: a whole 4x8x8 slice. The times are simulated.
512 devices in a mesh: row: 16 (over x, y_hi), col: 32 (over z, y_lo, core).
Axes of the slice: x: 4, y: 8 (y_hi: 4, y_lo: 2; y = y_hi * 2 + y_lo), z: 8, core: 2. Of those that a mesh axis runs over, the one named last changes fastest.
Arguments:
- left_factor: float32 [8192, 512], P(('row', 'col')), may hold values from -0.0625 to 0.0625
- left_cotangent: float32 [8192, 512], P(('row', 'col')), may hold values from -80 to 80
- right_factor: float32 [24576, 512], P(('col', 'row')), may hold values from -0.0390625 to 0.0390625
- right_cotangent: float32 [24576, 512], P(('col', 'row')), may hold values from -80 to 80
- singular: float32 [512], replicated, may hold values from 0.5 to 2, as said below
- singular_cotangent: float32 [512], replicated, may hold values from -384 to 384
Outputs:
- matrix_cotangent: float32 [8192, 24576], P('row', 'col')
Inputs may be any that keep to these rules, and one draw needn't show every extreme that they name: `singular`: strictly decreasing; consecutive values differ by at least 0.75 / 512.
All inputs are finite; a program needn't handle non-finite values.
Results may differ from a plain program's by a relative error of at most 0.0003.
Values sent between devices are 32-bit elements; how exact they have to be, the bound alone decides.
No kernel may reach another device: no remote copies, remote signals or barrier semaphores. Data moves between devices by JAX's collectives and lax.ppermute only.
A program may use at most 64 MiB of HBM per device.

v0:
```python
import jax
import jax.numpy as jnp
from jax import lax
from jax.sharding import PartitionSpec as P


def linear_core(gram_left, gram_right, singular):
    squares = singular * singular
    spread = squares[None, :] - squares[:, None]
    size_k = singular.shape[0]
    diagonal = jnp.eye(size_k, dtype=jnp.bool_)
    divided = jnp.where(
        diagonal, jnp.float32(0.0), 1.0 / jnp.where(diagonal, jnp.float32(1.0), spread)
    )
    inverse = 1.0 / singular
    core = divided * (gram_left - gram_left.T) * singular[None, :]
    core = core + singular[:, None] * (divided * (gram_right - gram_right.T))
    return core - gram_left * inverse[None, :] - inverse[:, None] * gram_right.T


def local(left_factor, left_cotangent, right_factor, right_cotangent, singular, singular_cotangent):
    highest = lax.Precision.HIGHEST
    dims = (((1,), (1,)), ((), ()))
    inverse = 1.0 / singular
    right_whole, right_cot_whole = (
        lax.all_gather(right_factor, "row", axis=0, tiled=True),
        lax.all_gather(right_cotangent, "row", axis=0, tiled=True),
    )
    scaled_right = right_cot_whole * inverse[None, :]
    local_left = jnp.dot(
        left_factor.T, left_cotangent, precision=highest, preferred_element_type=jnp.float32
    )
    local_right = jnp.dot(
        right_factor.T, right_cotangent, precision=highest, preferred_element_type=jnp.float32
    )
    gram_left, gram_right = lax.psum((local_left, local_right), ("row", "col"))
    core = linear_core(gram_left, gram_right, singular)
    core = core + jnp.diag(singular_cotangent)
    panel = (
        jnp.dot(left_factor, core, precision=highest, preferred_element_type=jnp.float32)
        + left_cotangent * inverse[None, :]
    )
    pieces = lax.all_gather((panel, left_factor), "col", axis=0, tiled=True)
    result = lax.dot_general(
        pieces[0], right_whole, dims, precision=highest, preferred_element_type=jnp.float32
    )
    return result + lax.dot_general(
        pieces[1], scaled_right, dims, precision=highest, preferred_element_type=jnp.float32
    )


def solution(mesh):
    placed = (
        P(("row", "col"), None),
        P(("row", "col"), None),
        P(("col", "row"), None),
        P(("col", "row"), None),
        P(),
        P(),
    )
    return jax.shard_map(
        local, mesh=mesh, in_specs=placed, out_specs=P("row", "col"), check_vma=False
    )
```

profile of v0, /device:TPU:1, one launch (start us, length us, event | category | flops | bytes accessed | tf_op | source)
XLA Modules:
  0.0 570.3 jit_solution(9918086712655896282)
XLA Ops:
  6.5 0.0 all-reduce.3.cloned.1.call-start
  6.5 2.8 fusion.31
  9.3 0.0 copy-start.4
  9.3 2.9 fusion.32
  12.3 0.0 all-reduce.3.cloned.1.call-update
  12.3 0.0 all-gather.11.cloned.1.call-start
  12.3 0.7 all-gather.11.cloned.1.call-update
  13.0 0.0 all-gather.9.cloned.1.call-start
  13.1 0.7 all-gather.9.cloned.1.call-update
  13.8 0.0 all-gather.7.cloned.1.call-start
  13.8 0.5 all-gather.7.cloned.1.call-update
  14.4 0.0 all-gather.5.cloned.1.call-start
  14.4 0.0 copy-done.4
  14.4 285.5 %all-reduce.3.cloned.1.call-done = (f32[512,512]{0,1:T(8,128)}, f32[512,512]{1,0:T(8,128)}) async-done(((f32[512,512]{0,1:T(8,128)}, f32[512,512]{1,0:T(8,128)}), (f32[512,512]{0,1:T(8,128)}, f32[512,512]{1,0:T(8,128)})) %all-reduce.3.cloned.1.call-update) | async-done | bytes 2097168 | tf_op jit(solution)/shard_map/psum | solution.py:36
  300.0 0.0 copy-start
  300.0 1.6 copy.7
  301.6 0.0 copy-start.1
  301.6 0.0 copy-start.2
  301.6 0.0 copy-start.3
  301.6 0.0 copy-start.5
  301.7 0.0 copy-done
  301.7 1.3 copy.9
  303.0 0.0 copy-done.1
  303.0 0.0 copy-done.2
  303.0 0.0 copy-done.3
  303.0 0.0 copy-done.5
  303.0 3.1 fusion.2
  306.1 0.0 all-gather.5.cloned.1.call-update
  306.1 59.1 %all-gather.11.cloned.1.call-done = f32[512,512]{1,0:T(8,128)} async-done(((f32[16,512]{1,0:T(8,128)}), f32[512,512]{1,0:T(8,128)}) %all-gather.11.cloned.1.call-update) | async-done | bytes 1048592 | tf_op jit(solution)/shard_map/all_gather | solution.py:43
  365.2 60.7 %all-gather.9.cloned.1.call-done = f32[768,512]{1,0:T(8,128)} async-done(((f32[48,512]{1,0:T(8,128)}), f32[768,512]{1,0:T(8,128)}) %all-gather.9.cloned.1.call-update) | async-done | bytes 1572880 | tf_op jit(solution)/shard_map/all_gather | solution.py:27
  425.9 4.4 fusion
  430.3 58.0 %all-gather.7.cloned.1.call-done = f32[768,512]{1,0:T(8,128)} async-done(((f32[48,512]{1,0:T(8,128)}), f32[768,512]{1,0:T(8,128)}) %all-gather.7.cloned.1.call-update) | async-done | bytes 1572880 | tf_op jit(solution)/shard_map/all_gather | solution.py:26
  488.3 69.9 %all-gather.5.cloned.1.call-done = f32[512,512]{1,0:T(8,128)} async-done(((f32[16,512]{1,0:T(8,128)}), f32[512,512]{1,0:T(8,128)}) %all-gather.5.cloned.1.call-update) | async-done | bytes 1048592 | tf_op jit(solution)/shard_map/all_gather | solution.py:43
  558.2 5.6 bitcast_add_fusion
  (1 shorter events, 0.0 us)
Async XLA Ops:
  6.5 293.4 %all-reduce.3.cloned.1.call-start = ((), (), s32[]{:S(2)}) async-start(), calls=%async_computation.4 | async-start | bytes 4194304 | tf_op jit(solution)/shard_map/psum | solution.py:36
  9.3 5.1 copy-start.4
  12.3 352.9 %all-gather.11.cloned.1.call-start = ((), (), s32[]{:S(2)}) async-start(), calls=%async_computation.3 | async-start | bytes 1081344 | tf_op jit(solution)/shard_map/all_gather | solution.py:43
  13.0 412.8 %all-gather.9.cloned.1.call-start = ((), (), s32[]{:S(2)}) async-start(), calls=%async_computation.2 | async-start | bytes 1671168 | tf_op jit(solution)/shard_map/all_gather | solution.py:27
  13.8 474.5 %all-gather.7.cloned.1.call-start = ((), (), s32[]{:S(2)}) async-start(), calls=%async_computation.1 | async-start | bytes 1671168 | tf_op jit(solution)/shard_map/all_gather | solution.py:26
  14.4 543.9 %all-gather.5.cloned.1.call-start = ((), (), s32[]{:S(2)}) async-start(), calls=%async_computation | async-start | bytes 1081344 | tf_op jit(solution)/shard_map/all_gather | solution.py:43
  300.0 1.7 copy-start
  301.6 1.4 copy-start.1
  301.6 1.4 copy-start.2
  301.6 1.3 copy-start.3
  301.6 1.3 copy-start.5
Sparse Core Ops, SparseCore 0:
  12.4 287.5 all-reduce.2
  302.1 63.0 all-gather.10
  368.3 57.5 all-gather.8
  428.8 59.4 all-gather.6
  490.3 67.9 all-gather.4
where the time goes:
time: 571 us; the launch traced here: 570 us
  waiting for transfers between devices  535 us (94%)
  matrix products  18.8 us (3%)
  between operations  13.2 us (2%)
    psum x1, waiting for transfers between devices, local(): gram_left, gram_right = lax.psum((local_left, local_right), ('row', 'col'))  286 us
    all_gather x2, waiting for transfers between devices, local(): pieces = lax.all_gather((panel, left_factor), 'col', axis=0, tiled=True)  129 us
    all_gather x1, waiting for transfers between devices, local(): lax.all_gather(right_cotangent, 'row', axis=0, tiled=True)  60.7 us
    all_gather x1, waiting for transfers between devices, local(): lax.all_gather(right_factor, 'row', axis=0, tiled=True)  58 us
  transfers between devices with their start and end apart: 5, of which 5 were waited for; matrix products, arithmetic and copies ran while one was open for 2% of the time, Pallas kernels for 0%

commit v1 on v0

--- a/solution.py
+++ b/solution.py
@@ -33,7 +33,7 @@
     local_right = jnp.dot(
         right_factor.T, right_cotangent, precision=highest, preferred_element_type=jnp.float32
     )
-    gram_left, gram_right = lax.psum((local_left, local_right), ("row", "col"))
+    gram_left, gram_right = lax.psum(lax.psum((local_left, local_right), "row"), "col")
     core = linear_core(gram_left, gram_right, singular)
     core = core + jnp.diag(singular_cotangent)
     panel = (

time: 571 us -> 716 us (1.25)
  waiting for transfers between devices: 535 us -> 680 us
    psum x1 -> x2, waiting for transfers between devices: 286 us -> 427 us  [the longest x1 246 us: local(): lax.psum(lax.psum((local_left, local_right), 'row'), 'col')]
  transfers between devices with their start and end apart: 5 -> 6, of which waited for: 5 -> 6; matrix products, arithmetic and copies ran while one was open for 2% -> 1% of each run, Pallas kernels for 0% -> 0%
where the time goes in v1:
time: 716 us; the launch traced here: 715 us
  waiting for transfers between devices  680 us (95%)
  matrix products  18.8 us (3%)
  between operations  13.6 us (2%)
    psum x1, waiting for transfers between devices, local(): lax.psum(lax.psum((local_left, local_right), 'row'), 'col')  246 us
    psum x1, waiting for transfers between devices, local(): lax.psum((local_left, local_right), 'row')  181 us
    all_gather x2, waiting for transfers between devices, local(): pieces = lax.all_gather((panel, left_factor), 'col', axis=0, tiled=True)  133 us
    all_gather x1, waiting for transfers between devices, local(): lax.all_gather(right_cotangent, 'row', axis=0, tiled=True)  60.5 us
    all_gather x1, waiting for transfers between devices, local(): lax.all_gather(right_factor, 'row', axis=0, tiled=True)  57.9 us
  transfers between devices with their start and end apart: 6, of which 6 were waited for; matrix products, arithmetic and copies ran while one was open for 1% of the time, Pallas kernels for 0%

profile of v1, /device:TPU:1, one launch (start us, length us, event | category | flops | bytes accessed | tf_op | source)
XLA Modules:
  0.0 715.5 jit_solution(16028343742845616542)
XLA Ops:
  6.5 0.0 all-reduce.7.cloned.1.call-start
  6.5 2.8 fusion.31
  9.3 2.9 fusion.32
  12.3 0.0 all-reduce.7.cloned.1.call-update
  12.3 0.0 copy-start.4
  12.3 0.0 all-reduce.5.cloned.1.call-start
  12.3 180.8 %all-reduce.7.cloned.1.call-done = (f32[512,512]{0,1:T(8,128)}, f32[512,512]{1,0:T(8,128)}) async-done(((f32[512,512]{0,1:T(8,128)}, f32[512,512]{1,0:T(8,128)}), (f32[512,512]{0,1:T(8,128)}, f32[512,512]{1,0:T(8,128)})) %all-reduce.7.cloned.1.call-update) | async-done | bytes 2097168 | tf_op jit(solution)/shard_map/psum | solution.py:36
  193.2 0.0 all-reduce.5.cloned.1.call-update
  193.2 0.0 all-gather.11.cloned.1.call-start
  193.3 0.7 all-gather.11.cloned.1.call-update
  194.0 0.0 all-gather.9.cloned.1.call-start
  194.0 0.5 all-gather.9.cloned.1.call-update
  194.5 0.0 all-gather.7.cloned.1.call-start
  194.6 0.5 all-gather.7.cloned.1.call-update
  195.1 0.0 all-gather.5.cloned.1.call-start
  195.2 0.0 copy-done.4
  195.2 246.1 %all-reduce.5.cloned.1.call-done = (f32[512,512]{0,1:T(8,128)}, f32[512,512]{1,0:T(8,128)}) async-done(((f32[512,512]{0,1:T(8,128)}, f32[512,512]{1,0:T(8,128)}), (f32[512,512]{0,1:T(8,128)}, f32[512,512]{1,0:T(8,128)})) %all-reduce.5.cloned.1.call-update) | async-done | bytes 2097168 | tf_op jit(solution)/shard_map/psum | solution.py:36
  441.3 0.0 copy-start
  441.3 1.6 copy.7
  442.9 0.0 copy-start.1
  442.9 0.0 copy-start.2
  442.9 0.0 copy-start.3
  443.0 0.0 copy-start.5
  443.0 0.0 copy-done
  443.0 1.3 copy.9
  444.3 0.0 copy-done.1
  444.3 0.0 copy-done.2
  444.3 0.0 copy-done.3
  444.3 0.0 copy-done.5
  444.3 3.1 fusion.2
  447.4 0.0 all-gather.5.cloned.1.call-update
  447.4 62.8 %all-gather.11.cloned.1.call-done = f32[512,512]{1,0:T(8,128)} async-done(((f32[16,512]{1,0:T(8,128)}), f32[512,512]{1,0:T(8,128)}) %all-gather.11.cloned.1.call-update) | async-done | bytes 1048592 | tf_op jit(solution)/shard_map/all_gather | solution.py:43
  510.2 60.5 %all-gather.9.cloned.1.call-done = f32[768,512]{1,0:T(8,128)} async-done(((f32[48,512]{1,0:T(8,128)}), f32[768,512]{1,0:T(8,128)}) %all-gather.9.cloned.1.call-update) | async-done | bytes 1572880 | tf_op jit(solution)/shard_map/all_gather | solution.py:27
  570.7 4.4 fusion
  575.1 57.9 %all-gather.7.cloned.1.call-done = f32[768,512]{1,0:T(8,128)} async-done(((f32[48,512]{1,0:T(8,128)}), f32[768,512]{1,0:T(8,128)}) %all-gather.7.cloned.1.call-update) | async-done | bytes 1572880 | tf_op jit(solution)/shard_map/all_gather | solution.py:26
  633.1 70.0 %all-gather.5.cloned.1.call-done = f32[512,512]{1,0:T(8,128)} async-done(((f32[16,512]{1,0:T(8,128)}), f32[512,512]{1,0:T(8,128)}) %all-gather.5.cloned.1.call-update) | async-done | bytes 1048592 | tf_op jit(solution)/shard_map/all_gather | solution.py:43
  703.0 5.6 bitcast_add_fusion
  (1 shorter events, 0.0 us)
Async XLA Ops:
  6.5 186.7 %all-reduce.7.cloned.1.call-start = ((), (), s32[]{:S(2)}) async-start(), calls=%async_computation.5 | async-start | bytes 4194304 | tf_op jit(solution)/shard_map/psum | solution.py:36
  12.3 182.9 %copy-start.4 = (f32[512]{0:T(512)S(1)}, f32[512]{0:T(512)}, u32[]{:S(2)}) copy-start(f32[512]{0:T(512)} %param.10) | copy-start | bytes 6148
  12.3 429.0 %all-reduce.5.cloned.1.call-start = ((), (), s32[]{:S(2)}) async-start(), calls=%async_computation.4 | async-start | bytes 4194304 | tf_op jit(solution)/shard_map/psum | solution.py:36
  193.2 317.0 %all-gather.11.cloned.1.call-start = ((), (), s32[]{:S(2)}) async-start(), calls=%async_computation.3 | async-start | bytes 1081344 | tf_op jit(solution)/shard_map/all_gather | solution.py:43
  194.0 376.7 %all-gather.9.cloned.1.call-start = ((), (), s32[]{:S(2)}) async-start(), calls=%async_computation.2 | async-start | bytes 1671168 | tf_op jit(solution)/shard_map/all_gather | solution.py:27
  194.5 438.5 %all-gather.7.cloned.1.call-start = ((), (), s32[]{:S(2)}) async-start(), calls=%async_computation.1 | async-start | bytes 1671168 | tf_op jit(solution)/shard_map/all_gather | solution.py:26
  195.1 507.9 %all-gather.5.cloned.1.call-start = ((), (), s32[]{:S(2)}) async-start(), calls=%async_computation | async-start | bytes 1081344 | tf_op jit(solution)/shard_map/all_gather | solution.py:43
  441.3 1.7 copy-start
  442.9 1.4 copy-start.1
  442.9 1.4 copy-start.2
  442.9 1.3 copy-start.3
  443.0 1.3 copy-start.5
Sparse Core Ops, SparseCore 0:
  12.4 180.7 all-reduce.6
  196.2 245.0 all-reduce.4
  443.4 66.6 all-gather.10
  513.1 57.5 all-gather.8
  573.6 59.4 all-gather.6
  635.1 67.9 all-gather.4
